TPU v7x, 256 devices: a whole 4x4x8 slice. The times are simulated.
256 devices in a mesh: pop: 32 (over x, y, core), site: 8 (over z).
Axes of the slice: x: 4, y: 4, z: 8, core: 2. Of those that a mesh axis runs over, the one named last changes fastest.
Arguments:
- profile: bfloat16 [32768, 96], P(('pop', 'site')), may hold values from 0 to 1
- panel: bfloat16 [32768, 128], P(('pop', 'site')), may hold values from -6 to 6
- visit_person: int32 [131072], P(('pop', 'site')), may hold values from 0 to 127
- visit_owner: int32 [131072], P(('pop', 'site')), may hold values from 0 to 31, as said below
- visit_row: int32 [131072], P(('pop', 'site')), may hold values from 0 to 1023, as said below
- visit_start: int32 [131072], P(('pop', 'site')), may hold values from 0 to 95
- visit_length: int32 [131072], P(('pop', 'site')), may hold values from 2 to 48
- tile_loc: int32 [2048], P(('pop', 'site')), may hold values from 0 to 7
Outputs:
- exposure: bfloat16 [32768, 128], P(('pop', 'site'))
Inputs may be any that keep to these rules, and one draw needn't show every extreme that they name: `visit_owner`: all devices with one site index send the same number of visits to a given owner index; at most 24 visits of one device go to one owner index, and in every draw some owner index receives exactly 24 from every device of a site index. `visit_row`: among the visits that reach one owner device the rows are distinct; in each tile the rows that are used come first and the rest are empty.
All inputs are finite; a program needn't handle non-finite values.
Results may differ from a plain program's by a relative error of at most 0.013.
Values may be sent and summed in bfloat16 or wider, within the bound.
No kernel may reach another device: no remote copies, remote signals or barrier semaphores. Data moves between devices by JAX's collectives and lax.ppermute only.
A program may use at most 64 MiB of HBM per device.

v0:
```python
import math
import jax
import jax.numpy as jnp
from jax import lax
from jax.sharding import PartitionSpec as P


def pair_terms(own_weights, own_places, running, pieces):
    far_weights, far_panel, far_places = pieces
    piece_tiles = far_weights.shape[0]
    group_size = math.gcd(piece_tiles, 8)
    group_count = piece_tiles // group_size
    grouped = (
        far_weights.reshape((group_count, group_size) + far_weights.shape[1:]),
        far_panel.reshape((group_count, group_size) + far_panel.shape[1:]),
        far_places.reshape(group_count, group_size),
    )

    def one_group(carried, item):
        group_weights, group_panel, group_places = item
        same_place = (own_places[:, None] == group_places[None, :]).astype(jnp.bfloat16)
        masked_far = group_weights[None, :, :, :] * same_place[:, :, None, None]
        copresence = jnp.einsum(
            "ars,abqs->abrq", own_weights, masked_far, preferred_element_type=jnp.float32
        )
        high_part = copresence.astype(jnp.bfloat16)
        low_part = (copresence - high_part.astype(jnp.float32)).astype(jnp.bfloat16)
        added = jnp.einsum(
            "abrq,bqc->arc", high_part, group_panel, preferred_element_type=jnp.float32
        )
        added = added + jnp.einsum(
            "abrq,bqc->arc", low_part, group_panel, preferred_element_type=jnp.float32
        )
        return (carried + added, None)

    result_sum, unused = lax.scan(one_group, running, grouped)
    return result_sum


def per_device(
    profile, panel, visit_person, visit_owner, visit_row, visit_start, visit_length, tile_loc
):
    pop_count = lax.axis_size("pop")
    visit_count = visit_person.shape[0]
    person_count, slot_count = profile.shape
    panel_width = panel.shape[1]
    capacity = visit_count // pop_count * 3 // 2
    tile_count = tile_loc.shape[0]
    row_count = tile_count * 128
    slot_ids = jnp.arange(slot_count, dtype=jnp.int32)
    finish = jnp.minimum(visit_start + visit_length, slot_count)
    inside = (slot_ids[None, :] >= visit_start[:, None]) & (slot_ids[None, :] < finish[:, None])
    weights = jnp.where(inside, profile[visit_person], jnp.zeros((), jnp.bfloat16))
    visit_panel = panel[visit_person]
    owner_hot = (visit_owner[:, None] == jnp.arange(pop_count, dtype=jnp.int32)[None, :]).astype(
        jnp.int32
    )
    position = jnp.sum((jnp.cumsum(owner_hot, axis=0) - 1) * owner_hot, axis=1)
    send_index = visit_owner * capacity + position
    send_weights = (
        jnp.zeros((pop_count * capacity, slot_count), jnp.bfloat16)
        .at[send_index]
        .set(weights)
        .reshape(pop_count, capacity, slot_count)
    )
    send_panel = (
        jnp.zeros((pop_count * capacity, panel_width), jnp.bfloat16)
        .at[send_index]
        .set(visit_panel)
        .reshape(pop_count, capacity, panel_width)
    )
    send_rows = (
        jnp.full((pop_count * capacity,), row_count, jnp.int32)
        .at[send_index]
        .set(visit_row)
        .reshape(pop_count, capacity)
    )
    got_weights, got_panel, got_rows = (
        lax.all_to_all(send_weights, "pop", split_axis=0, concat_axis=0, tiled=True),
        lax.all_to_all(send_panel, "pop", split_axis=0, concat_axis=0, tiled=True),
        lax.all_to_all(send_rows, "pop", split_axis=0, concat_axis=0, tiled=True),
    )
    target = got_rows.reshape(-1)
    tile_weights = (
        jnp.zeros((row_count, slot_count), jnp.bfloat16)
        .at[target]
        .set(got_weights.reshape(-1, slot_count), mode="drop")
        .reshape(tile_count, 128, slot_count)
    )
    tile_panel = (
        jnp.zeros((row_count, panel_width), jnp.bfloat16)
        .at[target]
        .set(got_panel.reshape(-1, panel_width), mode="drop")
        .reshape(tile_count, 128, panel_width)
    )
    initial = jnp.zeros((tile_count, 128, panel_width), jnp.float32)
    summed_rows = pair_terms(
        tile_weights,
        tile_loc,
        initial,
        (
            lax.all_gather(tile_weights, "site", axis=0, tiled=True),
            lax.all_gather(tile_panel, "site", axis=0, tiled=True),
            lax.all_gather(tile_loc, "site", axis=0, tiled=True),
        ),
    )
    row_result = (summed_rows / slot_count).astype(jnp.bfloat16).reshape(row_count, panel_width)
    sent_back = row_result[jnp.minimum(got_rows, row_count - 1)]
    returned = lax.all_to_all(sent_back, "pop", split_axis=0, concat_axis=0, tiled=True)
    own_results = returned.reshape(pop_count * capacity, panel_width)[send_index]
    person_hot = (
        jnp.arange(person_count, dtype=jnp.int32)[:, None] == visit_person[None, :]
    ).astype(jnp.bfloat16)
    return jnp.dot(person_hot, own_results, preferred_element_type=jnp.float32).astype(jnp.bfloat16)


def solution(mesh):
    placed = (
        P(("pop", "site"), None),
        P(("pop", "site"), None),
        P(("pop", "site")),
        P(("pop", "site")),
        P(("pop", "site")),
        P(("pop", "site")),
        P(("pop", "site")),
        P(("pop", "site")),
    )
    return jax.shard_map(
        per_device, mesh=mesh, in_specs=placed, out_specs=P(("pop", "site"), None), check_vma=False
    )
```

profile of v0, /device:TPU:1, one launch (start us, length us, event | category | flops | bytes accessed | tf_op | source)
XLA Modules:
  0.0 205.3 jit_solution(10561987336551839992)
XLA Ops:
  10.2 2.6 %scatter_custom_fusion = s32[768]{0:T(1024)S(1)} fusion(s32[512]{0:T(512)S(1)} %get-tuple-element.104, s32[512]{0:T(512)} %param.14, s32[]{:T(128)} %constant.8.clone.1), kind=kCustom, calls=%fused_computation.71 | custom fusion | bytes 3584 | tf_op jit(solution)/shard_map/scatter | solution.py:75
  13.5 8.6 %all-to-all-start = ((s32[32,1,24]{2,1,0:T(1,128)}), s32[32,1,24]{2,1,0:T(1,128)S(1)}, u32[]{:S(2)}, u32[]{:S(2)}) async-start(s32[32,1,24]{2,1,0:T(1,128)} %bitcast.2), calls=%async_computation | async-start | bytes 32768 | tf_op jit(solution)/shard_map/all_to_all | solution.py:81
  23.6 3.9 %scatter_custom_fusion.1 = bf16[768,96]{1,0:T(8,128)(2,1)} fusion(s32[512]{0:T(512)S(1)} %get-tuple-element.104, s32[512]{0:T(512)S(1)} %get-tuple-element.105, s32[512]{0:T(512)} %param.15, bf16[]{:T(256)} %constant.19.clone.1, bf16[128,96]{1,0:T(8,128)(2,1)S(1)} %copy.29, s32[1024]{0:T(1024)S(1)} %pad_clamp_fusion.2), kind=kCustom, calls=%fused_computation.40 | custom fusion | flops 196608 | bytes 189440 | tf_op jit(solution)/shard_map/scatter | solution.py:63
  28.9 6.0 %all-to-all-start.1 = ((bf16[32,24,96]{2,1,0:T(8,128)(2,1)}), bf16[32,24,96]{2,1,0:T(8,128)(2,1)S(1)}, u32[]{:S(2)}, u32[]{:S(2)}) async-start(bf16[32,24,96]{2,1,0:T(8,128)(2,1)} %bitcast.3), calls=%async_computation.1 | async-start | bytes 393216 | tf_op jit(solution)/shard_map/all_to_all | solution.py:79
  36.3 7.0 %all-to-all-done.1 = bf16[32,24,96]{2,1,0:T(8,128)(2,1)S(1)} async-done(((bf16[32,24,96]{2,1,0:T(8,128)(2,1)}), bf16[32,24,96]{2,1,0:T(8,128)(2,1)S(1)}, u32[]{:S(2)}, u32[]{:S(2)}) %all-to-all-start.1) | async-done | bytes 147488 | tf_op jit(solution)/shard_map/all_to_all | solution.py:79
  43.2 4.3 %scatter_custom_fusion.2 = bf16[1024,96]{1,0:T(8,128)(2,1)S(1)} fusion(s32[768]{0:T(1024)S(1)} %fusion.39, bf16[768,96]{1,0:T(8,128)(2,1)S(1)} %bitcast.114, bf16[]{:T(256)} %constant.19.clone.1), kind=kCustom, calls=%fused_computation.47 | custom fusion | bytes 196610 | tf_op jit(solution)/shard_map/scatter | solution.py:87
  48.5 3.0 %scatter_custom_fusion.3 = bf16[768,128]{1,0:T(8,128)(2,1)S(1)} fusion(s32[512]{0:T(512)S(1)} %get-tuple-element.104, bf16[128,128]{1,0:T(8,128)(2,1)S(1)} %copy-done, s32[1024]{0:T(1024)S(1)} %pad_clamp_fusion.2, bf16[]{:T(256)} %constant.19.clone.1), kind=kCustom, calls=%fused_computation.41 | custom fusion | bytes 196610 | tf_op jit(solution)/shard_map/scatter | solution.py:69
  51.5 11.9 %all_to_all.24 = bf16[32,24,128]{2,1,0:T(8,128)(2,1)S(1)} all-to-all(bf16[32,24,128]{2,1,0:T(8,128)(2,1)S(1)} %bitcast.112), channel_id=1, replica_groups=mesh['pop'=32,'site'=8] {'pop'}, dimensions={0} | all-to-all | bytes 393216 | tf_op jit(solution)/shard_map/all_to_all | solution.py:80
  63.4 4.9 %scatter_custom_fusion.4 = bf16[1024,128]{1,0:T(8,128)(2,1)} fusion(s32[768]{0:T(1024)S(1)} %fusion.39, bf16[768,128]{1,0:T(8,128)(2,1)S(1)} %bitcast.115, bf16[]{:T(256)} %constant.19.clone.1), kind=kCustom, calls=%fused_computation.43 | custom fusion | bytes 262146 | tf_op jit(solution)/shard_map/scatter | solution.py:93
  69.9 13.6 %all-reduce = s32[64]{0:T(128)S(1)} all-reduce(s32[64]{0:T(128)S(1)} %dynamic-update-slice), channel_id=1, replica_groups=mesh['pop'=32,'site'=8] {'site'}, use_global_device_ids=true, to_apply=%add | all-reduce | flops 64 | bytes 512
  83.9 3.5 %all-gather.3.cloned.1.call-done = bf16[64,128,96]{1,0,2:T(8,128)(2,1)} async-done(((bf16[8,128,96]{1,0,2:T(8,128)(2,1)}), bf16[64,128,96]{1,0,2:T(8,128)(2,1)}) %all-gather.3.cloned.1.call-update) | async-done | bytes 1572880 | tf_op jit(solution)/shard_map/all_gather | solution.py:102
  87.3 42.4 %all-gather.5.cloned.1.call-done = bf16[64,128,128]{2,1,0:T(8,128)(2,1)} async-done(((bf16[8,128,128]{2,1,0:T(8,128)(2,1)}), bf16[64,128,128]{2,1,0:T(8,128)(2,1)}) %all-gather.5.cloned.1.call-update) | async-done | bytes 2097168 | tf_op jit(solution)/shard_map/all_gather | solution.py:103
  129.7 44.4 %while.11 = (s32[]{:T(128)}, f32[8,128,128]{2,1,0:T(8,128)S(1)}, bf16[8,8,128,96]{2,1,0,3:T(8,128)(2,1)}, s32[8]{0:T(128)S(1)}, s32[8,8]{1,0:T(8,128)S(1)}, /*in...) while((s32[]{:T(128)}, f32[8,128,128]{2,1,0:T(8,128)S(1)}, ...), condition=%wide.region_9.10_spmd.clone, body=%wide.region_8.9_spmd.clone.sunk | while | flops 743571584 | bytes 16384511 | solution.py:36
  131.7 1.7 fusion.67
  133.4 1.9 fusion.68
  137.3 1.7 fusion.67
  139.0 1.9 fusion.68
  142.8 1.7 fusion.67
  144.5 1.9 fusion.68
  148.4 1.7 fusion.67
  150.1 1.9 fusion.68
  153.9 1.7 fusion.67
  155.6 1.9 fusion.68
  159.5 1.7 fusion.67
  161.2 1.9 fusion.68
  165.0 1.7 fusion.67
  166.7 1.9 fusion.68
  170.6 1.7 fusion.67
  172.3 1.9 fusion.68
  174.3 2.5 %gather_fusion = bf16[768,128]{1,0:T(8,128)(2,1)} fusion(bf16[1024,128]{1,0:T(8,128)(2,1)S(1)} %bitcast.106, s32[1024]{0:T(1024)S(1)} %pad_clamp_fusion.1), kind=kCustom, calls=%fused_computation.2 | custom fusion | bytes 396288 | tf_op jit(solution)/shard_map/gather | solution.py:108
  176.8 11.2 %all-to-all-start.3 = ((bf16[32,24,128]{2,1,0:T(8,128)(2,1)}), bf16[32,24,128]{2,1,0:T(8,128)(2,1)S(1)}, u32[]{:S(2)}, u32[]{:S(2)}) async-start(bf16[32,24,128]{2,1,0:T(8,128)(2,1)} %bitcast.14), calls=%async_computation.3 | async-start | bytes 393216 | tf_op jit(solution)/shard_map/all_to_all | solution.py:109
  188.0 8.3 %all-to-all-done.3 = bf16[32,24,128]{2,1,0:T(8,128)(2,1)S(1)} async-done(((bf16[32,24,128]{2,1,0:T(8,128)(2,1)}), bf16[32,24,128]{2,1,0:T(8,128)(2,1)S(1)}, u32[]{:S(2)}, u32[]{:S(2)}) %all-to-all-start.3) | async-done | bytes 196640 | tf_op jit(solution)/shard_map/all_to_all | solution.py:109
  (82 shorter events, 28.6 us)
Async XLA Ops:
  6.5 41.9 %copy-start = (bf16[128,128]{1,0:T(8,128)(2,1)S(1)}, bf16[128,128]{1,0:T(8,128)(2,1)}, u32[]{:S(2)}) copy-start(bf16[128,128]{1,0:T(8,128)(2,1)} %param.11) | copy-start | bytes 98308
  6.5 61.8 %copy-start.3 = (u32[256]{0:T(256)S(1)}, u32[256]{0:T(256)}, u32[]{:S(2)}) copy-start(u32[256]{0:T(256)} %constant.52) | copy-start | bytes 3076
  6.5 63.1 %copy-start.1 = (s32[8]{0:T(128)S(1)}, s32[8]{0:T(128)}, u32[]{:S(2)}) copy-start(s32[8]{0:T(128)} %param.17) | copy-start | bytes 100
  13.5 15.5 %all-to-all-start = ((s32[32,1,24]{2,1,0:T(1,128)}), s32[32,1,24]{2,1,0:T(1,128)S(1)}, u32[]{:S(2)}, u32[]{:S(2)}) async-start(s32[32,1,24]{2,1,0:T(1,128)} %bitcast.2), calls=%async_computation | async-start | bytes 32768 | tf_op jit(solution)/shard_map/all_to_all | solution.py:81
  28.9 14.3 %all-to-all-start.1 = ((bf16[32,24,96]{2,1,0:T(8,128)(2,1)}), bf16[32,24,96]{2,1,0:T(8,128)(2,1)S(1)}, u32[]{:S(2)}, u32[]{:S(2)}) async-start(bf16[32,24,96]{2,1,0:T(8,128)(2,1)} %bitcast.3), calls=%async_computation.1 | async-start | bytes 393216 | tf_op jit(solution)/shard_map/all_to_all | solution.py:79
  34.9 52.4 %all-gather.3.cloned.1.call-start = ((), (), s32[]{:S(2)}) async-start(), calls=%async_computation.4 | async-start | bytes 1769472 | tf_op jit(solution)/shard_map/all_gather | solution.py:102
  48.4 81.3 %all-gather.5.cloned.1.call-start = ((), (), s32[]{:S(2)}) async-start(), calls=%async_computation.5 | async-start | bytes 2359296 | tf_op jit(solution)/shard_map/all_gather | solution.py:103
  174.2 23.5 %copy-start.2 = (s32[512]{0:T(512)S(1)}, s32[512]{0:T(512)}, u32[]{:S(2)}) copy-start(s32[512]{0:T(512)} %param.12) | copy-start | bytes 6148
  176.8 19.6 %all-to-all-start.3 = ((bf16[32,24,128]{2,1,0:T(8,128)(2,1)}), bf16[32,24,128]{2,1,0:T(8,128)(2,1)S(1)}, u32[]{:S(2)}, u32[]{:S(2)}) async-start(bf16[32,24,128]{2,1,0:T(8,128)(2,1)} %bitcast.14), calls=%async_computation.3 | async-start | bytes 393216 | tf_op jit(solution)/shard_map/all_to_all | solution.py:109
Sparse Core Ops, SparseCore 0:
  48.5 38.7 all-gather.2
  89.1 40.5 all-gather.4
where the time goes:
time: 207 us; the launch traced here: 205 us
  waiting for transfers between devices  62.6 us (30%)
  matrix products  36.5 us (18%)
  local copies, waits for them, and re-layouts  30.9 us (15%)
  starting transfers between devices  25.9 us (13%)
  blocking collectives  25.5 us (12%)
  between operations  14.2 us (7%)
  other arithmetic  9.37 us (5%)
    all_gather x1, waiting for transfers between devices, per_device(): lax.all_gather(tile_panel, 'site', axis=0, tiled=True)  42.4 us
    dot_general x8, matrix products, one_group(): jnp.einsum('abrq,bqc->arc', high_part, group_panel, preferred_element_typ...  14.8 us
    unnamed x1, blocking collectives  13.6 us
    dot_general x8, matrix products, one_group(): jnp.einsum('abrq,bqc->arc', low_part, group_panel, preferred_element_type...  13.6 us
    all_to_all x1, blocking collectives, per_device(): lax.all_to_all(send_panel, 'pop', split_axis=0, concat_axis=0, tiled=True)  11.9 us
    all_to_all x1, starting transfers between devices, per_device(): lax.all_to_all(sent_back, 'pop', split_axis=0, concat_axis=0, tiled=True)  11.2 us
    all_to_all x1, starting transfers between devices, per_device(): lax.all_to_all(send_rows, 'pop', split_axis=0, concat_axis=0, tiled=True)  8.59 us
    all_to_all x1, waiting for transfers between devices, per_device(): lax.all_to_all(sent_back, 'pop', split_axis=0, concat_axis=0, tiled=True)  8.32 us
  transfers between devices with their start and end apart: 5, of which 5 were waited for; matrix products, arithmetic and copies ran while one was open for 8% of the time, Pallas kernels for 0%

commit v1 on v0

--- a/solution.py
+++ b/solution.py
@@ -100,7 +100,10 @@
         initial,
         (
             lax.all_gather(tile_weights, "site", axis=0, tiled=True),
-            lax.all_gather(tile_panel, "site", axis=0, tiled=True),
+            jnp.concatenate(
+                lax.all_to_all(jnp.stack([tile_panel] * lax.axis_size("site")), "site", 0, 0),
+                axis=0,
+            ),
             lax.all_gather(tile_loc, "site", axis=0, tiled=True),
         ),
     )

time: 207 us -> 192 us (0.928)
  waiting for transfers between devices: 62.6 us -> 27 us
  blocking collectives: 25.5 us -> 53.4 us
  matrix products: 36.5 us -> 21.2 us
  starting transfers between devices: 25.9 us -> 32.4 us
    all_gather x1 -> x0, waiting for transfers between devices: 42.4 us -> none  [per_device(): lax.all_gather(tile_panel, 'site', axis=0, tiled=True)]
    unnamed x1, blocking collectives: 13.6 us -> 53.4 us
    all_to_all x0 -> x2, starting transfers between devices: none -> 13.2 us  [the longest x1 8.32 us: per_device(): lax.all_to_all(jnp.stack([tile_panel] * lax.axis_size('site')), 'site', 0...]
    all_to_all x1 -> x0, blocking collectives: 11.9 us -> none  [per_device(): lax.all_to_all(send_panel, 'pop', split_axis=0, concat_axis=0, tiled=True)]
    dot_general x8, matrix products: 13.6 us -> 6.01 us  [one_group(): jnp.einsum('abrq,bqc->arc', low_part, group_panel, preferred_element_type...]
    dot_general x8, matrix products: 14.8 us -> 7.2 us  [one_group(): jnp.einsum('abrq,bqc->arc', high_part, group_panel, preferred_element_typ...]
    all_gather x1, waiting for transfers between devices: 3.46 us -> 9.78 us  [per_device(): lax.all_gather(tile_weights, 'site', axis=0, tiled=True)]
    all_to_all x1, starting transfers between devices: 11.2 us -> 6.65 us  [per_device(): lax.all_to_all(sent_back, 'pop', split_axis=0, concat_axis=0, tiled=True)]
  transfers between devices with their start and end apart: 5 -> 6, of which waited for: 5 -> 5; matrix products, arithmetic and copies ran while one was open for 8% -> 11% of each run, Pallas kernels for 0% -> 0%
where the time goes in v1:
time: 192 us; the launch traced here: 191 us
  blocking collectives  53.4 us (28%)
  local copies, waits for them, and re-layouts  32.8 us (17%)
  starting transfers between devices  32.4 us (17%)
  waiting for transfers between devices  27 us (14%)
  matrix products  21.2 us (11%)
  between operations  14.2 us (7%)
  other arithmetic  9.37 us (5%)
    unnamed x1, blocking collectives  53.4 us
    all_gather x1, waiting for transfers between devices, per_device(): lax.all_gather(tile_weights, 'site', axis=0, tiled=True)  9.78 us
    all_to_all x1, starting transfers between devices, per_device(): lax.all_to_all(send_rows, 'pop', split_axis=0, concat_axis=0, tiled=True)  8.59 us
    all_to_all x1, starting transfers between devices, per_device(): lax.all_to_all(jnp.stack([tile_panel] * lax.axis_size('site')), 'site', 0...  8.32 us
    all_to_all x1, waiting for transfers between devices, per_device(): lax.all_to_all(sent_back, 'pop', split_axis=0, concat_axis=0, tiled=True)  8.32 us
    dynamic_slice x16, local copies, waits for them, and re-layouts, pair_terms(): result_sum, unused = lax.scan(one_group, running, grouped)  7.75 us
    dot_general x8, matrix products, one_group(): jnp.einsum('ars,abqs->abrq', own_weights, masked_far, preferred_element_t...  7.23 us
    dot_general x8, matrix products, one_group(): jnp.einsum('abrq,bqc->arc', high_part, group_panel, preferred_element_typ...  7.2 us
  transfers between devices with their start and end apart: 6, of which 5 were waited for; matrix products, arithmetic and copies ran while one was open for 11% of the time, Pallas kernels for 0%

profile of v1, /device:TPU:1, one launch (start us, length us, event | category | flops | bytes accessed | tf_op | source)
XLA Modules:
  0.0 190.8 jit_solution(9617595420994793594)
XLA Ops:
  7.2 1.2 reduce-window.6
  10.2 2.6 %scatter_custom_fusion = s32[768]{0:T(1024)S(1)} fusion(s32[512]{0:T(512)S(1)} %get-tuple-element.104, s32[512]{0:T(512)} %param.14, s32[]{:T(128)} %constant.8.clone.1), kind=kCustom, calls=%fused_computation.71 | custom fusion | bytes 3584 | tf_op jit(solution)/shard_map/scatter | solution.py:75
  13.5 8.6 %all-to-all-start = ((s32[32,1,24]{2,1,0:T(1,128)}), s32[32,1,24]{2,1,0:T(1,128)S(1)}, u32[]{:S(2)}, u32[]{:S(2)}) async-start(s32[32,1,24]{2,1,0:T(1,128)} %bitcast.2), calls=%async_computation | async-start | bytes 32768 | tf_op jit(solution)/shard_map/all_to_all | solution.py:81
  22.8 3.6 %scatter_custom_fusion.3 = bf16[768,128]{1,0:T(8,128)(2,1)} fusion(s32[512]{0:T(512)S(1)} %get-tuple-element.104, bf16[128,128]{1,0:T(8,128)(2,1)S(1)} %copy-done, s32[1024]{0:T(1024)S(1)} %pad_clamp_fusion.2, bf16[]{:T(256)} %constant.19.clone.1), kind=kCustom, calls=%fused_computation.41 | custom fusion | bytes 196610 | tf_op jit(solution)/shard_map/scatter | solution.py:69
  26.4 2.5 %all-to-all-done = s32[32,1,24]{2,1,0:T(1,128)S(1)} async-done(((s32[32,1,24]{2,1,0:T(1,128)}), s32[32,1,24]{2,1,0:T(1,128)S(1)}, u32[]{:S(2)}, u32[]{:S(2)}) %all-to-all-start) | async-done | bytes 3104 | tf_op jit(solution)/shard_map/all_to_all | solution.py:81
  28.9 4.8 %all-to-all-start.2 = ((bf16[32,24,128]{2,1,0:T(8,128)(2,1)}), bf16[32,24,128]{2,1,0:T(8,128)(2,1)S(1)}, u32[]{:S(2)}, u32[]{:S(2)}) async-start(bf16[32,24,128]{2,1,0:T(8,128)(2,1)} %bitcast.8), calls=%async_computation.2 | async-start | bytes 393216 | tf_op jit(solution)/shard_map/all_to_all | solution.py:80
  34.6 3.9 %scatter_custom_fusion.1 = bf16[768,96]{1,0:T(8,128)(2,1)} fusion(s32[512]{0:T(512)S(1)} %get-tuple-element.104, s32[512]{0:T(512)S(1)} %get-tuple-element.105, s32[512]{0:T(512)} %param.15, bf16[]{:T(256)} %constant.19.clone.1, bf16[128,96]{1,0:T(8,128)(2,1)S(1)} %copy.29, s32[1024]{0:T(1024)S(1)} %pad_clamp_fusion.2), kind=kCustom, calls=%fused_computation.40 | custom fusion | flops 196608 | bytes 189440 | tf_op jit(solution)/shard_map/scatter | solution.py:63
  38.5 3.6 %all-to-all-done.2 = bf16[32,24,128]{2,1,0:T(8,128)(2,1)S(1)} async-done(((bf16[32,24,128]{2,1,0:T(8,128)(2,1)}), bf16[32,24,128]{2,1,0:T(8,128)(2,1)S(1)}, u32[]{:S(2)}, u32[]{:S(2)}) %all-to-all-start.2) | async-done | bytes 196640 | tf_op jit(solution)/shard_map/all_to_all | solution.py:80
  42.1 3.8 %all-to-all-start.1 = ((bf16[32,24,96]{2,1,0:T(8,128)(2,1)}), bf16[32,24,96]{2,1,0:T(8,128)(2,1)S(1)}, u32[]{:S(2)}, u32[]{:S(2)}) async-start(bf16[32,24,96]{2,1,0:T(8,128)(2,1)} %bitcast.3), calls=%async_computation.1 | async-start | bytes 393216 | tf_op jit(solution)/shard_map/all_to_all | solution.py:79
  47.3 4.3 %scatter_custom_fusion.4 = bf16[1024,128]{1,0:T(8,128)(2,1)S(1)} fusion(s32[768]{0:T(1024)S(1)} %fusion.39, bf16[768,128]{1,0:T(8,128)(2,1)S(1)} %bitcast.112, bf16[]{:T(256)} %constant.19.clone.1), kind=kCustom, calls=%fused_computation.43 | custom fusion | bytes 262146 | tf_op jit(solution)/shard_map/scatter | solution.py:93
  51.6 2.8 %all-to-all-done.1 = bf16[32,24,96]{2,1,0:T(8,128)(2,1)S(1)} async-done(((bf16[32,24,96]{2,1,0:T(8,128)(2,1)}), bf16[32,24,96]{2,1,0:T(8,128)(2,1)S(1)}, u32[]{:S(2)}, u32[]{:S(2)}) %all-to-all-start.1) | async-done | bytes 147488 | tf_op jit(solution)/shard_map/all_to_all | solution.py:79
  54.3 1.9 stack.3
  56.2 8.3 %all-to-all-start.3 = ((bf16[8,8,128,128]{3,2,1,0:T(8,128)(2,1)}), bf16[8,8,128,128]{3,2,1,0:T(8,128)(2,1)S(1)}, u32[]{:S(2)}, u32[]{:S(2)}) async-start(bf16[8,8,128,128]{3,2,1,0:T(8,128)(2,1)} %stack.3), calls=%async_computation.3 | async-start | bytes 4194304 | tf_op jit(solution)/shard_map/all_to_all | solution.py:104
  64.8 4.3 %scatter_custom_fusion.2 = bf16[1024,96]{1,0:T(8,128)(2,1)S(1)} fusion(s32[768]{0:T(1024)S(1)} %fusion.39, bf16[768,96]{1,0:T(8,128)(2,1)S(1)} %bitcast.111, bf16[]{:T(256)} %constant.19.clone.1), kind=kCustom, calls=%fused_computation.47 | custom fusion | bytes 196610 | tf_op jit(solution)/shard_map/scatter | solution.py:87
  71.5 53.4 %all-reduce = s32[64]{0:T(128)S(1)} all-reduce(s32[64]{0:T(128)S(1)} %dynamic-update-slice), channel_id=1, replica_groups=mesh['pop'=32,'site'=8] {'site'}, use_global_device_ids=true, to_apply=%add | all-reduce | flops 64 | bytes 512
  125.2 9.8 %all-gather.2.cloned.1.call-done = bf16[64,128,96]{1,0,2:T(8,128)(2,1)} async-done(((bf16[8,128,96]{1,0,2:T(8,128)(2,1)}), bf16[64,128,96]{1,0,2:T(8,128)(2,1)}) %all-gather.2.cloned.1.call-update) | async-done | bytes 1572880 | tf_op jit(solution)/shard_map/all_gather | solution.py:102
  135.0 29.2 %while.11 = (s32[]{:T(128)}, f32[8,128,128]{2,1,0:T(8,128)S(1)}, bf16[8,8,128,96]{2,1,0,3:T(8,128)(2,1)}, s32[8]{0:T(128)S(1)}, s32[8,8]{1,0:T(8,128)S(1)}, /*in...) while((s32[]{:T(128)}, f32[8,128,128]{2,1,0:T(8,128)S(1)}, ...), condition=%wide.region_9.10_spmd.clone, body=%wide.region_8.9_spmd.clone.sunk | while | flops 743571584 | bytes 16384511 | solution.py:36
  135.1 0.9 constant_dynamic-slice_fusion.3
  136.1 0.9 fusion.66
  138.8 0.9 constant_dynamic-slice_fusion.3
  139.7 0.9 fusion.66
  142.4 0.9 constant_dynamic-slice_fusion.3
  143.4 0.9 fusion.66
  146.1 0.9 constant_dynamic-slice_fusion.3
  149.7 0.9 constant_dynamic-slice_fusion.3
  153.4 0.9 constant_dynamic-slice_fusion.3
  157.0 0.9 constant_dynamic-slice_fusion.3
  160.7 0.9 constant_dynamic-slice_fusion.3
  164.3 2.5 %gather_fusion = bf16[768,128]{1,0:T(8,128)(2,1)} fusion(bf16[1024,128]{1,0:T(8,128)(2,1)S(1)} %bitcast.105, s32[1024]{0:T(1024)S(1)} %pad_clamp_fusion.1), kind=kCustom, calls=%fused_computation.2 | custom fusion | bytes 396288 | tf_op jit(solution)/shard_map/gather | solution.py:111
  166.8 6.6 %all-to-all-start.4 = ((bf16[32,24,128]{2,1,0:T(8,128)(2,1)}), bf16[32,24,128]{2,1,0:T(8,128)(2,1)S(1)}, u32[]{:S(2)}, u32[]{:S(2)}) async-start(bf16[32,24,128]{2,1,0:T(8,128)(2,1)} %bitcast.13), calls=%async_computation.4 | async-start | bytes 393216 | tf_op jit(solution)/shard_map/all_to_all | solution.py:112
  173.5 8.3 %all-to-all-done.4 = bf16[32,24,128]{2,1,0:T(8,128)(2,1)S(1)} async-done(((bf16[32,24,128]{2,1,0:T(8,128)(2,1)}), bf16[32,24,128]{2,1,0:T(8,128)(2,1)S(1)}, u32[]{:S(2)}, u32[]{:S(2)}) %all-to-all-start.4) | async-done | bytes 196640 | tf_op jit(solution)/shard_map/all_to_all | solution.py:112
  181.8 1.3 gather_fusion.1
  (83 shorter events, 27.8 us)
Async XLA Ops:
  6.5 16.2 %copy-start = (bf16[128,128]{1,0:T(8,128)(2,1)S(1)}, bf16[128,128]{1,0:T(8,128)(2,1)}, u32[]{:S(2)}) copy-start(bf16[128,128]{1,0:T(8,128)(2,1)} %param.11) | copy-start | bytes 98308
  13.5 15.5 %all-to-all-start = ((s32[32,1,24]{2,1,0:T(1,128)}), s32[32,1,24]{2,1,0:T(1,128)S(1)}, u32[]{:S(2)}, u32[]{:S(2)}) async-start(s32[32,1,24]{2,1,0:T(1,128)} %bitcast.2), calls=%async_computation | async-start | bytes 32768 | tf_op jit(solution)/shard_map/all_to_all | solution.py:81
  28.9 13.2 %all-to-all-start.2 = ((bf16[32,24,128]{2,1,0:T(8,128)(2,1)}), bf16[32,24,128]{2,1,0:T(8,128)(2,1)S(1)}, u32[]{:S(2)}, u32[]{:S(2)}) async-start(bf16[32,24,128]{2,1,0:T(8,128)(2,1)} %bitcast.8), calls=%async_computation.2 | async-start | bytes 393216 | tf_op jit(solution)/shard_map/all_to_all | solution.py:80
  42.1 12.2 %all-to-all-start.1 = ((bf16[32,24,96]{2,1,0:T(8,128)(2,1)}), bf16[32,24,96]{2,1,0:T(8,128)(2,1)S(1)}, u32[]{:S(2)}, u32[]{:S(2)}) async-start(bf16[32,24,96]{2,1,0:T(8,128)(2,1)} %bitcast.3), calls=%async_computation.1 | async-start | bytes 393216 | tf_op jit(solution)/shard_map/all_to_all | solution.py:79
  56.2 13.8 %copy-start.3 = (u32[256]{0:T(256)S(1)}, u32[256]{0:T(256)}, u32[]{:S(2)}) copy-start(u32[256]{0:T(256)} %constant.52) | copy-start | bytes 3076
  56.2 15.0 %copy-start.1 = (s32[8]{0:T(128)S(1)}, s32[8]{0:T(128)}, u32[]{:S(2)}) copy-start(s32[8]{0:T(128)} %param.17) | copy-start | bytes 100
  56.2 78.8 %all-to-all-start.3 = ((bf16[8,8,128,128]{3,2,1,0:T(8,128)(2,1)}), bf16[8,8,128,128]{3,2,1,0:T(8,128)(2,1)S(1)}, u32[]{:S(2)}, u32[]{:S(2)}) async-start(bf16[8,8,128,128]{3,2,1,0:T(8,128)(2,1)} %stack.3), calls=%async_computation.3 | async-start | bytes 4194304 | tf_op jit(solution)/shard_map/all_to_all | solution.py:104
  64.5 70.5 %all-gather.2.cloned.1.call-start = ((), (), s32[]{:S(2)}) async-start(), calls=%async_computation.5 | async-start | bytes 1769472 | tf_op jit(solution)/shard_map/all_gather | solution.py:102
  164.2 18.9 %copy-start.2 = (s32[512]{0:T(512)S(1)}, s32[512]{0:T(512)}, u32[]{:S(2)}) copy-start(s32[512]{0:T(512)} %param.12) | copy-start | bytes 6148
  166.8 15.0 %all-to-all-start.4 = ((bf16[32,24,128]{2,1,0:T(8,128)(2,1)}), bf16[32,24,128]{2,1,0:T(8,128)(2,1)S(1)}, u32[]{:S(2)}, u32[]{:S(2)}) async-start(bf16[32,24,128]{2,1,0:T(8,128)(2,1)} %bitcast.13), calls=%async_computation.4 | async-start | bytes 393216 | tf_op jit(solution)/shard_map/all_to_all | solution.py:112
Sparse Core Ops, SparseCore 0:
  70.1 64.8 all-gather.1
